TPU v7x, 256 devices: a whole 4x4x8 slice. The times are simulated.
256 devices in a mesh: slab: 8 (over x_lo, y), brick: 32 (over x_hi, z, core).
Axes of the slice: x: 4 (x_hi: 2, x_lo: 2; x = x_hi * 2 + x_lo), y: 4, z: 8, core: 2. Of those that a mesh axis runs over, the one named last changes fastest.
Arguments:
- embed: bfloat16 [262144, 512], P(('slab', 'brick')), may hold values from -6 to 6
- cotangent: bfloat16 [262144, 512], P(('slab', 'brick')), may hold values from -6 to 6
- basis: bfloat16 [16, 16, 262144], P(None, None, ('slab', 'brick')), may hold values from -4 to 4
- triplet_row_index: int32 [16, 262144], P(None, ('slab', 'brick')), may hold values from 0 to 1535
- triplet_slot_count: int32 [262144], P(('slab', 'brick')), may hold values from 1 to 16, as said below
- outgoing_edge_rows: int32 [4, 32768], P(None, ('slab', 'brick')), may hold values from 0 to 1023
- residual_weight: bfloat16 [512, 512], replicated, may hold values from -0.25 to 0.25
- down_weight: bfloat16 [512, 64], replicated, may hold values from -0.25 to 0.25
- up_weight: bfloat16 [64, 512], replicated, may hold values from -0.75 to 0.75
- basis_weight: bfloat16 [16, 64], replicated, may hold values from -1.5 to 1.5
Outputs:
- edge_embedding_gradient: bfloat16 [262144, 512], P(('slab', 'brick'))
- residual_weight_gradient: float32 [512, 512], replicated
- down_weight_gradient: float32 [512, 64], replicated
- up_weight_gradient: float32 [64, 512], replicated
- basis_weight_gradient: float32 [16, 64], replicated
Inputs may be any that keep to these rules, and one draw needn't show every extreme that they name: `triplet_row_index`: indices refer to the extended table of the edge's own brick. `triplet_slot_count`: slots at or past the count are empty; in every brick some edge fills all 16 slots; bricks differ in density. `outgoing_edge_rows`: local row numbers within the sending brick; a row may appear more than once.
All inputs are finite; a program needn't handle non-finite values.
Results may differ from a plain program's by a relative error of at most 0.006.
Values may be sent and summed in bfloat16 or wider, within the bound.
A program may use at most 64 MiB of HBM per device.

v0:
```python
import jax
import jax.numpy as jnp
from jax import lax
from jax.sharding import PartitionSpec as P


def passed_along(value, axis, steps):
    count = lax.axis_size(axis)
    pairs = [(source, (source + steps) % count) for source in range(count)]
    return lax.ppermute(value, axis, pairs)


def silu_grad(value):
    sig = jax.nn.sigmoid(value)
    return sig * (1.0 + value * (1.0 - sig))


def selector(index_row, count_rows, dtype):
    positions = lax.broadcasted_iota(jnp.int32, (count_rows, index_row.shape[0]), 0)
    return (positions == index_row[None, :]).astype(dtype)


def shards(
    embed,
    cotangent,
    basis,
    triplet_row_index,
    triplet_slot_count,
    outgoing_edge_rows,
    residual_weight,
    down_weight,
    up_weight,
    basis_weight,
):
    rows = embed.shape[0]
    ghost = outgoing_edge_rows.shape[1]
    trips = triplet_row_index.shape[0]
    res_pre = jnp.dot(embed, residual_weight, preferred_element_type=jnp.float32)
    dres = (cotangent.astype(jnp.float32) * silu_grad(res_pre)).astype(jnp.bfloat16)
    residual_weight_gradient = lax.dot_general(
        embed, dres, (((0,), (0,)), ((), ())), preferred_element_type=jnp.float32
    )
    res_term = lax.dot_general(
        dres, residual_weight, (((1,), (1,)), ((), ())), preferred_element_type=jnp.float32
    )
    pre = lax.dot_general(
        down_weight, embed, (((0,), (1,)), ((), ())), preferred_element_type=jnp.float32
    )
    proj = jax.nn.silu(pre).astype(jnp.bfloat16)
    picks = [selector(outgoing_edge_rows[step], rows, jnp.bfloat16) for step in range(4)]
    received = []
    for step, by in enumerate((1, -1)):
        chosen = jnp.dot(proj, picks[step], preferred_element_type=jnp.float32).astype(jnp.bfloat16)
        received.append(passed_along(chosen, "slab", by))
    for step, by in enumerate((1, -1)):
        chosen = jnp.dot(proj, picks[step + 2], preferred_element_type=jnp.float32).astype(
            jnp.bfloat16
        )
        received.append(passed_along(chosen, "brick", by))
    ghost_proj = jnp.concatenate(received, axis=1)
    edge_table_rows = jnp.concatenate([proj, ghost_proj], axis=1)
    table_rows = edge_table_rows.shape[1]
    weight_list = jnp.einsum("unz,nh->uhz", basis, basis_weight, preferred_element_type=jnp.float32)
    live = (lax.broadcasted_iota(jnp.int32, (trips, rows), 0) < triplet_slot_count[None, :]).astype(
        jnp.float32
    )

    def gather_slot(carry, index_row):
        onehot = selector(index_row, table_rows, jnp.bfloat16)
        picked = jnp.dot(edge_table_rows, onehot, preferred_element_type=jnp.float32).astype(
            jnp.bfloat16
        )
        return (carry, picked)

    _, gathered = lax.scan(gather_slot, jnp.zeros((), jnp.float32), triplet_row_index)
    gathered = gathered.astype(jnp.float32)
    tsum = jnp.sum(weight_list * gathered * live[:, None, :], axis=0)
    activation_value = jax.nn.silu(tsum).astype(jnp.bfloat16)
    dsum = lax.dot_general(
        up_weight, cotangent, (((1,), (1,)), ((), ())), preferred_element_type=jnp.float32
    )
    dt = dsum * silu_grad(tsum)
    up_weight_gradient = lax.dot_general(
        activation_value, cotangent, (((1,), (0,)), ((), ())), preferred_element_type=jnp.float32
    )
    weight_gradient_list = (dt[None, :, :] * gathered * live[:, None, :]).astype(jnp.bfloat16)
    basis_weight_gradient = jnp.einsum(
        "yqi,ywi->qw", basis, weight_gradient_list, preferred_element_type=jnp.float32
    )
    dhx = dt[None, :, :] * weight_list * live[:, None, :]

    def scatter_slot(total, inputs):
        index_row, slot_terms = inputs
        onehot = selector(index_row, table_rows, jnp.float32)
        added = lax.dot_general(
            slot_terms,
            onehot,
            (((1,), (1,)), ((), ())),
            precision=lax.Precision.HIGHEST,
            preferred_element_type=jnp.float32,
        )
        return (total + added, None)

    table_gradient, _ = lax.scan(
        scatter_slot,
        jnp.zeros((edge_table_rows.shape[0], table_rows), jnp.float32),
        (triplet_row_index, dhx),
    )
    dproj = table_gradient[:, :rows]
    for step, by in enumerate((1, -1)):
        block = table_gradient[:, rows + step * ghost : rows + (step + 1) * ghost]
        back = passed_along(block, "slab", -by)
        dproj = dproj + lax.dot_general(
            back,
            picks[step].astype(jnp.float32),
            (((1,), (1,)), ((), ())),
            precision=lax.Precision.HIGHEST,
            preferred_element_type=jnp.float32,
        )
    for step, by in enumerate((1, -1)):
        block = table_gradient[:, rows + (step + 2) * ghost : rows + (step + 3) * ghost]
        back = passed_along(block, "brick", -by)
        dproj = dproj + lax.dot_general(
            back,
            picks[step + 2].astype(jnp.float32),
            (((1,), (1,)), ((), ())),
            precision=lax.Precision.HIGHEST,
            preferred_element_type=jnp.float32,
        )
    dpre = (dproj * silu_grad(pre)).astype(jnp.bfloat16)
    down_weight_gradient = lax.dot_general(
        embed, dpre, (((0,), (1,)), ((), ())), preferred_element_type=jnp.float32
    )
    down_term = lax.dot_general(
        dpre, down_weight, (((0,), (1,)), ((), ())), preferred_element_type=jnp.float32
    )
    edge_embedding_gradient = (res_term + down_term).astype(jnp.bfloat16)
    reduced_total = lax.psum(
        (residual_weight_gradient, down_weight_gradient, up_weight_gradient, basis_weight_gradient),
        ("slab", "brick"),
    )
    return (
        edge_embedding_gradient,
        reduced_total[0],
        reduced_total[1],
        reduced_total[2],
        reduced_total[3],
    )


def solution(mesh):
    in_specs = (
        P(("slab", "brick"), None),
        P(("slab", "brick"), None),
        P(None, None, ("slab", "brick")),
        P(None, ("slab", "brick")),
        P(("slab", "brick")),
        P(None, ("slab", "brick")),
        P(),
        P(),
        P(),
        P(),
    )
    out_specs = (P(("slab", "brick"), None), P(), P(), P(), P())
    return jax.shard_map(shards, mesh=mesh, in_specs=in_specs, out_specs=out_specs, check_vma=False)
```

profile of v0, /device:TPU:2, one launch (start us, length us, event | category | flops | bytes accessed | tf_op | source)
XLA Modules:
  0.0 442.0 jit_solution(11072315548361697162)
XLA Ops:
  16.3 6.4 %collective-permute-start.3 = (bf16[64,128]{1,0:T(8,128)(2,1)S(1)}, bf16[64,128]{1,0:T(8,128)(2,1)S(1)}, u32[]{:S(2)}, u32[]{:S(2)}) collective-permute-start(bf16[64,128]{1,0:T(8,128)(2,1)S(1)} %convolution_convert_fusion), channel_id=1, source_target_pairs={{0,31},{1,0},{2,1},{3,2},{4,3},{5,4},{6,5},{7,6},{8,7},{9,8},{10,9... | collective-permute-start | bytes 49160 | tf_op jit(solution)/shard_map/ppermute | solution.py:10
  25.9 30.5 %while.21 = (s32[]{:T(128)}, bf16[16,64,1024]{2,1,0:T(8,128)(2,1)S(1)}, s32[16,1024]{1,0:T(8,128)}, bf16[64,1536]{1,0:T(8,128)(2,1)S(1)}, s32[]{:T(128)}) while((s32[]{:T(128)}, bf16[16,64,1024]{2,1,0:T(8,128)(2,1)S(1)}, s32[16,1024]{1,0:T(8,128)}, bf16[64,1536]{1,0:T(8,128)(2,1)S(1)}, s32[]{:T(128)}) %tuple.49), condition=%wide.region_1.2_spmd, body=%wide.region_0.1_spmd.sunk | while | flops 202964992 | bytes 340037 | solution.py:75
  59.2 2.9 fusion.15
  62.1 93.6 %while.22 = (s32[]{:T(128)}, f32[64,1536]{1,0:T(8,128)}, f32[16,64,1024]{2,1,0:T(8,128)}, s32[16,1024]{1,0:T(8,128)}, s32[]{:T(128)}, /*index=5*/s32[]{:T(128)}) while((s32[]{:T(128)}, f32[64,1536]{1,0:T(8,128)}, f32[16,64,1024]{2,1,0:T(8,128)}, s32[16,1024]{1,0:T(8,128)}, s32[]{:T(128)}, /*index=5*/s32[]{:T(128)}) %tuple.59), condition=%wide.region_4.5_spmd.clone, body=%wide.region_3.4_spmd.clone.sunk | while | flops 1209729024 | bytes 1061459 | solution.py:104
  62.9 5.0 %fusion.80 = f32[64,1536]{1,0:T(8,128)} fusion(s32[1024]{0:T(1024)S(1)} %bitcast.73, f32[64,1536]{1,0:T(8,128)} %get-tuple-element.175, f32[16,64,1024]{2,1,0:T(8,128)} %get-tuple-element.182, s32[]{:T(128)} %get-tuple-element.174, pred[]{:T(512)S(6)} %compare.3), kind=kOutput, calls=%fused_computation.10.clone.1 | convolution fusion | flops 1209729024 | bytes 1053185 | tf_op jit(solution)/shard_map/while/body/eval_jaxpr/dot_general | solution.py:95
  68.6 5.1 %fusion.80 = f32[64,1536]{1,0:T(8,128)} fusion(s32[1024]{0:T(1024)S(1)} %bitcast.73, f32[64,1536]{1,0:T(8,128)} %get-tuple-element.175, f32[16,64,1024]{2,1,0:T(8,128)} %get-tuple-element.182, s32[]{:T(128)} %get-tuple-element.174, pred[]{:T(512)S(6)} %compare.3), kind=kOutput, calls=%fused_computation.10.clone.1 | convolution fusion | flops 1209729024 | bytes 1053185 | tf_op jit(solution)/shard_map/while/body/eval_jaxpr/dot_general | solution.py:95
  74.5 5.1 %fusion.80 = f32[64,1536]{1,0:T(8,128)} fusion(s32[1024]{0:T(1024)S(1)} %bitcast.73, f32[64,1536]{1,0:T(8,128)} %get-tuple-element.175, f32[16,64,1024]{2,1,0:T(8,128)} %get-tuple-element.182, s32[]{:T(128)} %get-tuple-element.174, pred[]{:T(512)S(6)} %compare.3), kind=kOutput, calls=%fused_computation.10.clone.1 | convolution fusion | flops 1209729024 | bytes 1053185 | tf_op jit(solution)/shard_map/while/body/eval_jaxpr/dot_general | solution.py:95
  80.4 5.1 %fusion.80 = f32[64,1536]{1,0:T(8,128)} fusion(s32[1024]{0:T(1024)S(1)} %bitcast.73, f32[64,1536]{1,0:T(8,128)} %get-tuple-element.175, f32[16,64,1024]{2,1,0:T(8,128)} %get-tuple-element.182, s32[]{:T(128)} %get-tuple-element.174, pred[]{:T(512)S(6)} %compare.3), kind=kOutput, calls=%fused_computation.10.clone.1 | convolution fusion | flops 1209729024 | bytes 1053185 | tf_op jit(solution)/shard_map/while/body/eval_jaxpr/dot_general | solution.py:95
  86.2 5.1 %fusion.80 = f32[64,1536]{1,0:T(8,128)} fusion(s32[1024]{0:T(1024)S(1)} %bitcast.73, f32[64,1536]{1,0:T(8,128)} %get-tuple-element.175, f32[16,64,1024]{2,1,0:T(8,128)} %get-tuple-element.182, s32[]{:T(128)} %get-tuple-element.174, pred[]{:T(512)S(6)} %compare.3), kind=kOutput, calls=%fused_computation.10.clone.1 | convolution fusion | flops 1209729024 | bytes 1053185 | tf_op jit(solution)/shard_map/while/body/eval_jaxpr/dot_general | solution.py:95
  92.1 5.1 %fusion.80 = f32[64,1536]{1,0:T(8,128)} fusion(s32[1024]{0:T(1024)S(1)} %bitcast.73, f32[64,1536]{1,0:T(8,128)} %get-tuple-element.175, f32[16,64,1024]{2,1,0:T(8,128)} %get-tuple-element.182, s32[]{:T(128)} %get-tuple-element.174, pred[]{:T(512)S(6)} %compare.3), kind=kOutput, calls=%fused_computation.10.clone.1 | convolution fusion | flops 1209729024 | bytes 1053185 | tf_op jit(solution)/shard_map/while/body/eval_jaxpr/dot_general | solution.py:95
  97.9 5.1 %fusion.80 = f32[64,1536]{1,0:T(8,128)} fusion(s32[1024]{0:T(1024)S(1)} %bitcast.73, f32[64,1536]{1,0:T(8,128)} %get-tuple-element.175, f32[16,64,1024]{2,1,0:T(8,128)} %get-tuple-element.182, s32[]{:T(128)} %get-tuple-element.174, pred[]{:T(512)S(6)} %compare.3), kind=kOutput, calls=%fused_computation.10.clone.1 | convolution fusion | flops 1209729024 | bytes 1053185 | tf_op jit(solution)/shard_map/while/body/eval_jaxpr/dot_general | solution.py:95
  103.8 5.1 %fusion.80 = f32[64,1536]{1,0:T(8,128)} fusion(s32[1024]{0:T(1024)S(1)} %bitcast.73, f32[64,1536]{1,0:T(8,128)} %get-tuple-element.175, f32[16,64,1024]{2,1,0:T(8,128)} %get-tuple-element.182, s32[]{:T(128)} %get-tuple-element.174, pred[]{:T(512)S(6)} %compare.3), kind=kOutput, calls=%fused_computation.10.clone.1 | convolution fusion | flops 1209729024 | bytes 1053185 | tf_op jit(solution)/shard_map/while/body/eval_jaxpr/dot_general | solution.py:95
  109.6 5.1 %fusion.80 = f32[64,1536]{1,0:T(8,128)} fusion(s32[1024]{0:T(1024)S(1)} %bitcast.73, f32[64,1536]{1,0:T(8,128)} %get-tuple-element.175, f32[16,64,1024]{2,1,0:T(8,128)} %get-tuple-element.182, s32[]{:T(128)} %get-tuple-element.174, pred[]{:T(512)S(6)} %compare.3), kind=kOutput, calls=%fused_computation.10.clone.1 | convolution fusion | flops 1209729024 | bytes 1053185 | tf_op jit(solution)/shard_map/while/body/eval_jaxpr/dot_general | solution.py:95
  115.5 5.1 %fusion.80 = f32[64,1536]{1,0:T(8,128)} fusion(s32[1024]{0:T(1024)S(1)} %bitcast.73, f32[64,1536]{1,0:T(8,128)} %get-tuple-element.175, f32[16,64,1024]{2,1,0:T(8,128)} %get-tuple-element.182, s32[]{:T(128)} %get-tuple-element.174, pred[]{:T(512)S(6)} %compare.3), kind=kOutput, calls=%fused_computation.10.clone.1 | convolution fusion | flops 1209729024 | bytes 1053185 | tf_op jit(solution)/shard_map/while/body/eval_jaxpr/dot_general | solution.py:95
  121.4 5.1 %fusion.80 = f32[64,1536]{1,0:T(8,128)} fusion(s32[1024]{0:T(1024)S(1)} %bitcast.73, f32[64,1536]{1,0:T(8,128)} %get-tuple-element.175, f32[16,64,1024]{2,1,0:T(8,128)} %get-tuple-element.182, s32[]{:T(128)} %get-tuple-element.174, pred[]{:T(512)S(6)} %compare.3), kind=kOutput, calls=%fused_computation.10.clone.1 | convolution fusion | flops 1209729024 | bytes 1053185 | tf_op jit(solution)/shard_map/while/body/eval_jaxpr/dot_general | solution.py:95
  127.2 5.1 %fusion.80 = f32[64,1536]{1,0:T(8,128)} fusion(s32[1024]{0:T(1024)S(1)} %bitcast.73, f32[64,1536]{1,0:T(8,128)} %get-tuple-element.175, f32[16,64,1024]{2,1,0:T(8,128)} %get-tuple-element.182, s32[]{:T(128)} %get-tuple-element.174, pred[]{:T(512)S(6)} %compare.3), kind=kOutput, calls=%fused_computation.10.clone.1 | convolution fusion | flops 1209729024 | bytes 1053185 | tf_op jit(solution)/shard_map/while/body/eval_jaxpr/dot_general | solution.py:95
  133.1 5.1 %fusion.80 = f32[64,1536]{1,0:T(8,128)} fusion(s32[1024]{0:T(1024)S(1)} %bitcast.73, f32[64,1536]{1,0:T(8,128)} %get-tuple-element.175, f32[16,64,1024]{2,1,0:T(8,128)} %get-tuple-element.182, s32[]{:T(128)} %get-tuple-element.174, pred[]{:T(512)S(6)} %compare.3), kind=kOutput, calls=%fused_computation.10.clone.1 | convolution fusion | flops 1209729024 | bytes 1053185 | tf_op jit(solution)/shard_map/while/body/eval_jaxpr/dot_general | solution.py:95
  138.9 5.1 %fusion.80 = f32[64,1536]{1,0:T(8,128)} fusion(s32[1024]{0:T(1024)S(1)} %bitcast.73, f32[64,1536]{1,0:T(8,128)} %get-tuple-element.175, f32[16,64,1024]{2,1,0:T(8,128)} %get-tuple-element.182, s32[]{:T(128)} %get-tuple-element.174, pred[]{:T(512)S(6)} %compare.3), kind=kOutput, calls=%fused_computation.10.clone.1 | convolution fusion | flops 1209729024 | bytes 1053185 | tf_op jit(solution)/shard_map/while/body/eval_jaxpr/dot_general | solution.py:95
  144.8 5.1 %fusion.80 = f32[64,1536]{1,0:T(8,128)} fusion(s32[1024]{0:T(1024)S(1)} %bitcast.73, f32[64,1536]{1,0:T(8,128)} %get-tuple-element.175, f32[16,64,1024]{2,1,0:T(8,128)} %get-tuple-element.182, s32[]{:T(128)} %get-tuple-element.174, pred[]{:T(512)S(6)} %compare.3), kind=kOutput, calls=%fused_computation.10.clone.1 | convolution fusion | flops 1209729024 | bytes 1053185 | tf_op jit(solution)/shard_map/while/body/eval_jaxpr/dot_general | solution.py:95
  150.7 5.1 %fusion.80 = f32[64,1536]{1,0:T(8,128)} fusion(s32[1024]{0:T(1024)S(1)} %bitcast.73, f32[64,1536]{1,0:T(8,128)} %get-tuple-element.175, f32[16,64,1024]{2,1,0:T(8,128)} %get-tuple-element.182, s32[]{:T(128)} %get-tuple-element.174, pred[]{:T(512)S(6)} %compare.3), kind=kOutput, calls=%fused_computation.10.clone.1 | convolution fusion | flops 1209729024 | bytes 1053185 | tf_op jit(solution)/shard_map/while/body/eval_jaxpr/dot_general | solution.py:95
  156.6 3.7 collective-permute-start.6
  162.5 4.1 collective-permute-start.4
  173.2 76.4 %psum.31 = f32[16,64]{1,0:T(8,128)} all-reduce(f32[16,64]{1,0:T(8,128)S(1)} %fusion.25), channel_id=1, replica_groups=mesh['slab'=8,'brick'=32] {'slab','brick'}, use_global_device_ids=true, to_apply=%region_8.9 | all-reduce | flops 1024 | bytes 8192 | tf_op jit(solution)/shard_map/psum | solution.py:138
  251.8 179.5 %all-reduce.3.cloned.1.call-done = (f32[512,512]{0,1:T(8,128)}, f32[512,64]{0,1:T(8,128)}, f32[64,512]{1,0:T(8,128)}) async-done(((f32[512,512]{0,1:T(8,128)}, f32[512,64]{0,1:T(8,128)}, f32[64,512]{1,0:T(8,128)}), (f32[512,512]{0,1:T(8,128)}, f32[512,64]{0,1:T(8,128)}, f32[64,512]{1,0:T(8,128)})) %all-reduce.3.cloned.1.call-update) | async-done | bytes 1310736 | tf_op jit(solution)/shard_map/psum | solution.py:138
  (125 shorter events, 73.1 us)
Async XLA Ops:
  7.2 15.5 %copy-start.12 = (bf16[1024,512]{1,0:T(8,128)(2,1)S(1)}, bf16[1024,512]{1,0:T(8,128)(2,1)}, u32[]{:S(2)}) copy-start(bf16[1024,512]{1,0:T(8,128)(2,1)} %param.15) | copy-start | bytes 3145732
  7.2 15.5 %copy-start.3 = (bf16[512,512]{1,0:T(8,128)(2,1)S(1)}, bf16[512,512]{1,0:T(8,128)(2,1)}, u32[]{:S(2)}) copy-start(bf16[512,512]{1,0:T(8,128)(2,1)} %param.20) | copy-start | bytes 1572868
  7.2 424.1 %all-reduce.3.cloned.1.call-start = ((), (), s32[]{:S(2)}) async-start(), calls=%async_computation | async-start | bytes 2621440 | tf_op jit(solution)/shard_map/psum | solution.py:138
  11.3 14.5 %collective-permute-start = (bf16[64,128]{1,0:T(8,128)(2,1)}, bf16[64,128]{1,0:T(8,128)(2,1)S(1)}, u32[]{:S(2)}, u32[]{:S(2)}) collective-permute-start(bf16[64,128]{1,0:T(8,128)(2,1)} %convolution_convert_fusion.3), channel_id=1, source_target_pairs={{0,32},{32,64},{64,96},{96,128},{128,160},{160,192},{192,224},{224... | collective-permute-start | bytes 49160 | tf_op jit(solution)/shard_map/ppermute | solution.py:10
  13.1 12.7 %collective-permute-start.1 = (bf16[64,128]{1,0:T(8,128)(2,1)S(1)}, bf16[64,128]{1,0:T(8,128)(2,1)S(1)}, u32[]{:S(2)}, u32[]{:S(2)}) collective-permute-start(bf16[64,128]{1,0:T(8,128)(2,1)S(1)} %convolution_convert_fusion.2), channel_id=1, source_target_pairs={{0,224},{32,0},{64,32},{96,64},{128,96},{160,128},{192,160},{224,1... | collective-permute-start | bytes 49160 | tf_op jit(solution)/shard_map/ppermute | solution.py:10
  16.0 9.9 %collective-permute-start.2 = (bf16[64,128]{1,0:T(8,128)(2,1)S(1)}, bf16[64,128]{1,0:T(8,128)(2,1)S(1)}, u32[]{:S(2)}, u32[]{:S(2)}) collective-permute-start(bf16[64,128]{1,0:T(8,128)(2,1)S(1)} %convolution_convert_fusion.1), channel_id=1, source_target_pairs={{0,1},{1,2},{2,3},{3,4},{4,5},{5,6},{6,7},{7,8},{8,9},{9,10},{10,1... | collective-permute-start | bytes 49160 | tf_op jit(solution)/shard_map/ppermute | solution.py:10
  16.3 9.5 %collective-permute-start.3 = (bf16[64,128]{1,0:T(8,128)(2,1)S(1)}, bf16[64,128]{1,0:T(8,128)(2,1)S(1)}, u32[]{:S(2)}, u32[]{:S(2)}) collective-permute-start(bf16[64,128]{1,0:T(8,128)(2,1)S(1)} %convolution_convert_fusion), channel_id=1, source_target_pairs={{0,31},{1,0},{2,1},{3,2},{4,3},{5,4},{6,5},{7,6},{8,7},{9,8},{10,9... | collective-permute-start | bytes 49160 | tf_op jit(solution)/shard_map/ppermute | solution.py:10
  24.0 1.8 copy-start.1
  24.0 1.8 copy-start.11
  25.9 30.5 %copy-start.10 = (bf16[16,64]{1,0:T(8,128)(2,1)S(1)}, bf16[16,64]{1,0:T(8,128)(2,1)}, u32[]{:S(2)}) copy-start(bf16[16,64]{1,0:T(8,128)(2,1)} %param.23) | copy-start | bytes 6148
  56.4 2.3 copy-start.13
  56.4 2.3 copy-start.14
  59.2 2.9 copy-start.5
  155.7 14.1 %copy-start.9 = (f32[64,1536]{1,0:T(8,128)S(1)}, f32[64,1536]{1,0:T(8,128)}, u32[]{:S(2)}) copy-start(f32[64,1536]{1,0:T(8,128)} %get-tuple-element.50) | copy-start | bytes 1179652
  155.8 14.1 %copy-start.15 = (f32[64,1024]{1,0:T(8,128)S(1)}, f32[64,1024]{1,0:T(8,128)}, u32[]{:S(2)}) copy-start(f32[64,1024]{1,0:T(8,128)} %get-tuple-element.100) | copy-start | bytes 786436
  156.6 10.0 %collective-permute-start.6 = (f32[64,128]{1,0:T(8,128)S(1)}, f32[64,128]{1,0:T(8,128)S(1)}, u32[]{:S(2)}, u32[]{:S(2)}) collective-permute-start(f32[64,128]{1,0:T(8,128)S(1)} %get-tuple-element.95), channel_id=1, source_target_pairs={{0,31},{1,0},{2,1},{3,2},{4,3},{5,4},{6,5},{7,6},{8,7},{9,8},{10,9... | collective-permute-start | bytes 98312 | tf_op jit(solution)/shard_map/ppermute | solution.py:10
  162.5 6.0 %collective-permute-start.5 = (f32[64,128]{1,0:T(8,128)S(1)}, f32[64,128]{1,0:T(8,128)S(1)}, u32[]{:S(2)}, u32[]{:S(2)}) collective-permute-start(f32[64,128]{1,0:T(8,128)S(1)} %get-tuple-element.93), channel_id=1, source_target_pairs={{0,32},{32,64},{64,96},{96,128},{128,160},{160,192},{192,224},{224... | collective-permute-start | bytes 98312 | tf_op jit(solution)/shard_map/ppermute | solution.py:10
  162.5 7.0 %collective-permute-start.7 = (f32[64,128]{1,0:T(8,128)S(1)}, f32[64,128]{1,0:T(8,128)S(1)}, u32[]{:S(2)}, u32[]{:S(2)}) collective-permute-start(f32[64,128]{1,0:T(8,128)S(1)} %get-tuple-element.94), channel_id=1, source_target_pairs={{0,1},{1,2},{2,3},{3,4},{4,5},{5,6},{6,7},{7,8},{8,9},{9,10},{10,1... | collective-permute-start | bytes 98312 | tf_op jit(solution)/shard_map/ppermute | solution.py:10
  162.5 7.4 %collective-permute-start.4 = (f32[64,128]{1,0:T(8,128)S(1)}, f32[64,128]{1,0:T(8,128)S(1)}, u32[]{:S(2)}, u32[]{:S(2)}) collective-permute-start(f32[64,128]{1,0:T(8,128)S(1)} %get-tuple-element.92), channel_id=1, source_target_pairs={{0,224},{32,0},{64,32},{96,64},{128,96},{160,128},{192,160},{224,1... | collective-permute-start | bytes 98312 | tf_op jit(solution)/shard_map/ppermute | solution.py:10
  171.3 78.2 %copy-start.8 = (bf16[512,64]{0,1:T(8,128)(2,1)S(1)}, bf16[512,64]{0,1:T(8,128)(2,1)}, u32[]{:S(2)}) copy-start(bf16[512,64]{0,1:T(8,128)(2,1)} %param.21) | copy-start | bytes 196612
  173.2 76.9 %copy-start.2 = (bf16[1024,512]{1,0:T(8,128)(2,1)S(1)}, bf16[1024,512]{1,0:T(8,128)(2,1)}, u32[]{:S(2)}) copy-start(bf16[1024,512]{1,0:T(8,128)(2,1)} %copy-done.1) | copy-start | bytes 3145732
  173.2 76.9 %copy-start.4 = (bf16[512,512]{1,0:T(8,128)(2,1)S(1)}, bf16[512,512]{1,0:T(8,128)(2,1)}, u32[]{:S(2)}) copy-start(bf16[512,512]{1,0:T(8,128)(2,1)} %param.20) | copy-start | bytes 1572868
  431.3 2.6 copy-start.7
  431.3 3.2 copy-start.6
  (1 other events, 1.3 us)
Sparse Core Ops, SparseCore 0:
  171.5 259.7 all-reduce.2
where the time goes:
time: 445 us; the launch traced here: 442 us
  waiting for transfers between devices  182 us (41%)
  matrix products  117 us (26%)
  blocking collectives  76.4 us (17%)
  local copies, waits for them, and re-layouts  30.6 us (7%)
  starting transfers between devices  18.5 us (4%)
  between operations  14.3 us (3%)
    psum x1, waiting for transfers between devices, shards(): lax.psum((residual_weight_gradient, down_weight_gradient, up_weight_gradi...  179 us
    dot_general x16, matrix products, scatter_slot(): lax.dot_general(slot_terms, onehot, (((1,), (1,)), ((), ())), precision=l...  81.4 us
    psum x1, blocking collectives, shards(): lax.psum((residual_weight_gradient, down_weight_gradient, up_weight_gradi...  76.4 us
    dynamic_slice x32, local copies, waits for them, and re-layouts, shards(): lax.scan(gather_slot, jnp.zeros((), jnp.float32), triplet_row_index)  24.5 us
    ppermute x8, starting transfers between devices, passed_along(): return lax.ppermute(value, axis, pairs)  18.5 us
    dot_general x16, matrix products, gather_slot(): jnp.dot(edge_table_rows, onehot, preferred_element_type=jnp.float32)  18 us
  transfers between devices with their start and end apart: 9, of which 3 were waited for; matrix products, arithmetic and copies ran while one was open for 3% of the time, Pallas kernels for 0%

commit v1 on v0

--- a/solution.py
+++ b/solution.py
@@ -135,9 +135,14 @@
         dpre, down_weight, (((0,), (1,)), ((), ())), preferred_element_type=jnp.float32
     )
     edge_embedding_gradient = (res_term + down_term).astype(jnp.bfloat16)
-    reduced_total = lax.psum(
-        (residual_weight_gradient, down_weight_gradient, up_weight_gradient, basis_weight_gradient),
-        ("slab", "brick"),
+
+    def _report_numbers(xs):
+        for jj in ("slab", "brick"):
+            xs = jax.lax.psum(xs, jj)
+        return xs
+
+    reduced_total = _report_numbers(
+        (residual_weight_gradient, down_weight_gradient, up_weight_gradient, basis_weight_gradient)
     )
     return (
         edge_embedding_gradient,

time: 445 us -> 541 us (1.22)
  waiting for transfers between devices: 182 us -> 267 us
  blocking collectives: 76.4 us -> 85 us
    psum x1 -> x2, waiting for transfers between devices: 179 us -> 265 us  [_report_numbers(): xs = jax.lax.psum(xs, jj)]
    psum x1 -> x2, blocking collectives: 76.4 us -> 85 us  [_report_numbers(): xs = jax.lax.psum(xs, jj)]
  transfers between devices with their start and end apart: 9 -> 10, of which waited for: 3 -> 4; matrix products, arithmetic and copies ran while one was open for 3% -> 2% of each run, Pallas kernels for 0% -> 0%
where the time goes in v1:
time: 541 us; the launch traced here: 536 us
  waiting for transfers between devices  267 us (49%)
  matrix products  117 us (22%)
  blocking collectives  85 us (16%)
  local copies, waits for them, and re-layouts  30.6 us (6%)
  starting transfers between devices  18.6 us (3%)
  between operations  14.3 us (3%)
    psum x2, waiting for transfers between devices, _report_numbers(): xs = jax.lax.psum(xs, jj)  265 us
    psum x2, blocking collectives, _report_numbers(): xs = jax.lax.psum(xs, jj)  85 us
    dot_general x16, matrix products, scatter_slot(): lax.dot_general(slot_terms, onehot, (((1,), (1,)), ((), ())), precision=l...  81.4 us
    dynamic_slice x32, local copies, waits for them, and re-layouts, shards(): lax.scan(gather_slot, jnp.zeros((), jnp.float32), triplet_row_index)  24.5 us
    ppermute x8, starting transfers between devices, passed_along(): return lax.ppermute(value, axis, pairs)  18.5 us
    dot_general x16, matrix products, gather_slot(): jnp.dot(edge_table_rows, onehot, preferred_element_type=jnp.float32)  18 us
  transfers between devices with their start and end apart: 10, of which 4 were waited for; matrix products, arithmetic and copies ran while one was open for 2% of the time, Pallas kernels for 0%

profile of v1, /device:TPU:2, one launch (start us, length us, event | category | flops | bytes accessed | tf_op | source)
XLA Modules:
  0.0 536.3 jit_solution(492509099226611664)
XLA Ops:
  16.3 6.4 %collective-permute-start.3 = (bf16[64,128]{1,0:T(8,128)(2,1)S(1)}, bf16[64,128]{1,0:T(8,128)(2,1)S(1)}, u32[]{:S(2)}, u32[]{:S(2)}) collective-permute-start(bf16[64,128]{1,0:T(8,128)(2,1)S(1)} %convolution_convert_fusion), channel_id=1, source_target_pairs={{0,31},{1,0},{2,1},{3,2},{4,3},{5,4},{6,5},{7,6},{8,7},{9,8},{10,9... | collective-permute-start | bytes 49160 | tf_op jit(solution)/shard_map/ppermute | solution.py:10
  25.9 30.5 %while.21 = (s32[]{:T(128)}, bf16[16,64,1024]{2,1,0:T(8,128)(2,1)S(1)}, s32[16,1024]{1,0:T(8,128)}, bf16[64,1536]{1,0:T(8,128)(2,1)S(1)}, s32[]{:T(128)}) while((s32[]{:T(128)}, bf16[16,64,1024]{2,1,0:T(8,128)(2,1)S(1)}, s32[16,1024]{1,0:T(8,128)}, bf16[64,1536]{1,0:T(8,128)(2,1)S(1)}, s32[]{:T(128)}) %tuple.49), condition=%wide.region_1.2_spmd, body=%wide.region_0.1_spmd.sunk | while | flops 202964992 | bytes 340037 | solution.py:75
  62.1 93.6 %while.22 = (s32[]{:T(128)}, f32[64,1536]{1,0:T(8,128)}, f32[16,64,1024]{2,1,0:T(8,128)}, s32[16,1024]{1,0:T(8,128)}, s32[]{:T(128)}, /*index=5*/s32[]{:T(128)}) while((s32[]{:T(128)}, f32[64,1536]{1,0:T(8,128)}, f32[16,64,1024]{2,1,0:T(8,128)}, s32[16,1024]{1,0:T(8,128)}, s32[]{:T(128)}, /*index=5*/s32[]{:T(128)}) %tuple.62), condition=%wide.region_4.5_spmd.clone, body=%wide.region_3.4_spmd.clone.sunk | while | flops 1209729024 | bytes 1061459 | solution.py:104
  62.9 5.0 fusion.80
  68.6 5.1 fusion.80
  74.5 5.1 fusion.80
  80.3 5.1 fusion.80
  86.2 5.1 fusion.80
  92.0 5.1 fusion.80
  97.9 5.1 fusion.80
  103.8 5.1 fusion.80
  109.6 5.1 fusion.80
  115.5 5.1 fusion.80
  121.3 5.1 fusion.80
  127.2 5.1 fusion.80
  133.0 5.1 fusion.80
  138.9 5.1 fusion.80
  144.8 5.1 fusion.80
  150.6 5.1 fusion.80
  162.5 4.1 collective-permute-start.4
  171.4 80.5 %all-reduce.7.cloned.1.call-done = (f32[512,512]{0,1:T(8,128)}, f32[512,64]{0,1:T(8,128)}, f32[64,512]{1,0:T(8,128)}) async-done(((f32[512,512]{0,1:T(8,128)}, f32[512,64]{0,1:T(8,128)}, f32[64,512]{1,0:T(8,128)}), (f32[512,512]{0,1:T(8,128)}, f32[512,64]{0,1:T(8,128)}, f32[64,512]{1,0:T(8,128)})) %all-reduce.7.cloned.1.call-update) | async-done | bytes 1310736 | tf_op jit(solution)/shard_map/psum | solution.py:141
  253.7 18.3 %psum.62 = f32[16,64]{1,0:T(8,128)S(1)} all-reduce(f32[16,64]{1,0:T(8,128)S(1)} %fusion.25), channel_id=1, replica_groups=mesh['slab'=8,'brick'=32] {'slab'}, use_global_device_ids=true, to_apply=%region_11.12 | all-reduce | flops 1024 | bytes 8192 | tf_op jit(solution)/shard_map/psum | solution.py:141
  272.0 66.7 %psum.63 = f32[16,64]{1,0:T(8,128)} all-reduce(f32[16,64]{1,0:T(8,128)S(1)} %psum.62), channel_id=1, replica_groups=mesh['slab'=8,'brick'=32] {'brick'}, use_global_device_ids=true, to_apply=%region_12.13 | all-reduce | flops 1024 | bytes 8192 | tf_op jit(solution)/shard_map/psum | solution.py:141
  340.9 184.7 %all-reduce.5.cloned.1.call-done = (f32[512,512]{0,1:T(8,128)}, f32[512,64]{0,1:T(8,128)}, f32[64,512]{1,0:T(8,128)}) async-done(((f32[512,512]{0,1:T(8,128)}, f32[512,64]{0,1:T(8,128)}, f32[64,512]{1,0:T(8,128)}), (f32[512,512]{0,1:T(8,128)}, f32[512,64]{0,1:T(8,128)}, f32[64,512]{1,0:T(8,128)})) %all-reduce.5.cloned.1.call-update) | async-done | bytes 1310736 | tf_op jit(solution)/shard_map/psum | solution.py:141
  (129 shorter events, 79.7 us)
Async XLA Ops:
  7.2 15.5 %copy-start.12 = (bf16[1024,512]{1,0:T(8,128)(2,1)S(1)}, bf16[1024,512]{1,0:T(8,128)(2,1)}, u32[]{:S(2)}) copy-start(bf16[1024,512]{1,0:T(8,128)(2,1)} %param.15) | copy-start | bytes 3145732
  7.2 15.5 %copy-start.3 = (bf16[512,512]{1,0:T(8,128)(2,1)S(1)}, bf16[512,512]{1,0:T(8,128)(2,1)}, u32[]{:S(2)}) copy-start(bf16[512,512]{1,0:T(8,128)(2,1)} %param.20) | copy-start | bytes 1572868
  7.2 244.6 %all-reduce.7.cloned.1.call-start = ((), (), s32[]{:S(2)}) async-start(), calls=%async_computation.1 | async-start | bytes 2621440 | tf_op jit(solution)/shard_map/psum | solution.py:141
  11.3 14.5 %collective-permute-start = (bf16[64,128]{1,0:T(8,128)(2,1)}, bf16[64,128]{1,0:T(8,128)(2,1)S(1)}, u32[]{:S(2)}, u32[]{:S(2)}) collective-permute-start(bf16[64,128]{1,0:T(8,128)(2,1)} %convolution_convert_fusion.3), channel_id=1, source_target_pairs={{0,32},{32,64},{64,96},{96,128},{128,160},{160,192},{192,224},{224... | collective-permute-start | bytes 49160 | tf_op jit(solution)/shard_map/ppermute | solution.py:10
  13.1 12.7 %collective-permute-start.1 = (bf16[64,128]{1,0:T(8,128)(2,1)S(1)}, bf16[64,128]{1,0:T(8,128)(2,1)S(1)}, u32[]{:S(2)}, u32[]{:S(2)}) collective-permute-start(bf16[64,128]{1,0:T(8,128)(2,1)S(1)} %convolution_convert_fusion.2), channel_id=1, source_target_pairs={{0,224},{32,0},{64,32},{96,64},{128,96},{160,128},{192,160},{224,1... | collective-permute-start | bytes 49160 | tf_op jit(solution)/shard_map/ppermute | solution.py:10
  16.0 9.8 %collective-permute-start.2 = (bf16[64,128]{1,0:T(8,128)(2,1)S(1)}, bf16[64,128]{1,0:T(8,128)(2,1)S(1)}, u32[]{:S(2)}, u32[]{:S(2)}) collective-permute-start(bf16[64,128]{1,0:T(8,128)(2,1)S(1)} %convolution_convert_fusion.1), channel_id=1, source_target_pairs={{0,1},{1,2},{2,3},{3,4},{4,5},{5,6},{6,7},{7,8},{8,9},{9,10},{10,1... | collective-permute-start | bytes 49160 | tf_op jit(solution)/shard_map/ppermute | solution.py:10
  16.3 9.5 %collective-permute-start.3 = (bf16[64,128]{1,0:T(8,128)(2,1)S(1)}, bf16[64,128]{1,0:T(8,128)(2,1)S(1)}, u32[]{:S(2)}, u32[]{:S(2)}) collective-permute-start(bf16[64,128]{1,0:T(8,128)(2,1)S(1)} %convolution_convert_fusion), channel_id=1, source_target_pairs={{0,31},{1,0},{2,1},{3,2},{4,3},{5,4},{6,5},{7,6},{8,7},{9,8},{10,9... | collective-permute-start | bytes 49160 | tf_op jit(solution)/shard_map/ppermute | solution.py:10
  24.0 1.7 copy-start.1
  25.9 30.5 %copy-start.10 = (bf16[16,64]{1,0:T(8,128)(2,1)S(1)}, bf16[16,64]{1,0:T(8,128)(2,1)}, u32[]{:S(2)}) copy-start(bf16[16,64]{1,0:T(8,128)(2,1)} %param.23) | copy-start | bytes 6148
  56.4 2.3 copy-start.13
  56.4 2.3 copy-start.14
  59.2 2.9 copy-start.5
  155.7 14.1 %copy-start.9 = (f32[64,1536]{1,0:T(8,128)S(1)}, f32[64,1536]{1,0:T(8,128)}, u32[]{:S(2)}) copy-start(f32[64,1536]{1,0:T(8,128)} %get-tuple-element.50) | copy-start | bytes 1179652
  155.7 14.1 %copy-start.15 = (f32[64,1024]{1,0:T(8,128)S(1)}, f32[64,1024]{1,0:T(8,128)}, u32[]{:S(2)}) copy-start(f32[64,1024]{1,0:T(8,128)} %get-tuple-element.103) | copy-start | bytes 786436
  156.6 10.0 %collective-permute-start.6 = (f32[64,128]{1,0:T(8,128)S(1)}, f32[64,128]{1,0:T(8,128)S(1)}, u32[]{:S(2)}, u32[]{:S(2)}) collective-permute-start(f32[64,128]{1,0:T(8,128)S(1)} %get-tuple-element.98), channel_id=1, source_target_pairs={{0,31},{1,0},{2,1},{3,2},{4,3},{5,4},{6,5},{7,6},{8,7},{9,8},{10,9... | collective-permute-start | bytes 98312 | tf_op jit(solution)/shard_map/ppermute | solution.py:10
  162.5 6.0 %collective-permute-start.5 = (f32[64,128]{1,0:T(8,128)S(1)}, f32[64,128]{1,0:T(8,128)S(1)}, u32[]{:S(2)}, u32[]{:S(2)}) collective-permute-start(f32[64,128]{1,0:T(8,128)S(1)} %get-tuple-element.96), channel_id=1, source_target_pairs={{0,32},{32,64},{64,96},{96,128},{128,160},{160,192},{192,224},{224... | collective-permute-start | bytes 98312 | tf_op jit(solution)/shard_map/ppermute | solution.py:10
  162.5 7.0 %collective-permute-start.7 = (f32[64,128]{1,0:T(8,128)S(1)}, f32[64,128]{1,0:T(8,128)S(1)}, u32[]{:S(2)}, u32[]{:S(2)}) collective-permute-start(f32[64,128]{1,0:T(8,128)S(1)} %get-tuple-element.97), channel_id=1, source_target_pairs={{0,1},{1,2},{2,3},{3,4},{4,5},{5,6},{6,7},{7,8},{8,9},{9,10},{10,1... | collective-permute-start | bytes 98312 | tf_op jit(solution)/shard_map/ppermute | solution.py:10
  162.5 7.4 %collective-permute-start.4 = (f32[64,128]{1,0:T(8,128)S(1)}, f32[64,128]{1,0:T(8,128)S(1)}, u32[]{:S(2)}, u32[]{:S(2)}) collective-permute-start(f32[64,128]{1,0:T(8,128)S(1)} %get-tuple-element.95), channel_id=1, source_target_pairs={{0,224},{32,0},{64,32},{96,64},{128,96},{160,128},{192,160},{224,1... | collective-permute-start | bytes 98312 | tf_op jit(solution)/shard_map/ppermute | solution.py:10
  171.3 354.3 %all-reduce.5.cloned.1.call-start = ((), (), s32[]{:S(2)}) async-start(), calls=%async_computation | async-start | bytes 2621440 | tf_op jit(solution)/shard_map/psum | solution.py:141
  251.9 86.8 %copy-start.8 = (bf16[512,64]{0,1:T(8,128)(2,1)S(1)}, bf16[512,64]{0,1:T(8,128)(2,1)}, u32[]{:S(2)}) copy-start(bf16[512,64]{0,1:T(8,128)(2,1)} %param.21) | copy-start | bytes 196612
  253.7 85.5 %copy-start.2 = (bf16[1024,512]{1,0:T(8,128)(2,1)S(1)}, bf16[1024,512]{1,0:T(8,128)(2,1)}, u32[]{:S(2)}) copy-start(bf16[1024,512]{1,0:T(8,128)(2,1)} %copy-done.1) | copy-start | bytes 3145732
  253.7 85.5 %copy-start.4 = (bf16[512,512]{1,0:T(8,128)(2,1)S(1)}, bf16[512,512]{1,0:T(8,128)(2,1)}, u32[]{:S(2)}) copy-start(bf16[512,512]{1,0:T(8,128)(2,1)} %param.20) | copy-start | bytes 1572868
  525.6 2.6 copy-start.7
  525.6 3.2 copy-start.6
  (2 other events, 3.0 us)
Sparse Core Ops, SparseCore 0:
  171.5 80.3 all-reduce.6
  254.7 270.8 all-reduce.4
